TPU v7x, 32 devices: a whole 2x2x4 slice. The times are simulated.
32 devices in a mesh: groups: 2 (over y), sub: 16 (over z, x, core).
Axes of the slice: x: 2, y: 2, z: 4, core: 2. Of those that a mesh axis runs over, the one named last changes fastest.
Arguments:
- samples: bfloat16 [16896, 512], P(('groups', 'sub')), parts along dimension 0, may hold values from -6 to 6
- channel_order: int32 [512], replicated, may hold values from 0 to 511, each once
- merge_table: int32 [9, 3, 256], replicated, may hold values from 0 to 128, as said below
Outputs:
- spectra: float32 [512, 4096], P(('groups', 'sub')), parts along dimension 0
There are 2 independent parts, one for each index of `groups`. A program takes and returns all parts, laid end to end along the dimension named above; an argument that names none is the same for every part. Nothing has to cross between parts.
Inputs may be any that keep to these rules, and one draw needn't show every extreme that they name: `channel_order`: a permutation of the 512 channels. `merge_table`: for level l, entry j is row d = j % 2**(l-1) of merged subband j // 2**(l-1); with C = max(1, 2**(l-2)) and e = 8, entries 0 and 1 lie in [e * (d // (2 e)), e * (d // (2 e)) + min(C, e)), and entry 2 equals entry 0 or entry 0 plus 1.
All inputs are finite; a program needn't handle non-finite values.
Results may differ from a plain program's by a relative error of at most 0.012.
Values may be sent and summed in bfloat16 or wider, within the bound.
No kernel may reach another device: no remote copies, remote signals or barrier semaphores. Data moves between devices by JAX's collectives and lax.ppermute only.
A program may use at most 64 MiB of HBM per device.

v0:
```python
import math
import jax
import jax.numpy as jnp
from jax import lax
from jax.sharding import PartitionSpec as P

LOCAL = 5
CH_DEV = 32
SAMPLES = 8192


def from_partner(block, axis, apart):
    count = lax.axis_size(axis)
    route = []
    for low in range(count):
        high = low | 1 << apart
        if high != low and high < count:
            route += [(low, high), (high, low)]
    return lax.ppermute(block, axis, route)


def delay_rows(values, shifts, margin, time_axis):
    length = values.shape[time_axis]
    moved = values
    for bit_num in range(max(1, margin.bit_length())):
        offset = 2**bit_num
        rolled = jnp.pad(moved[:, offset:], ((0, 0), (0, offset)))
        flagged = shifts >> bit_num & 1 == 1
        flagged = flagged[:, None]
        moved = jnp.where(flagged, rolled, moved)
    return moved


def merge_level(current, entries, child_rows, span_rows, time_axis):
    outputs = jnp.arange(entries.shape[1], dtype=jnp.int32)
    starts = 2 * child_rows * (outputs // span_rows)
    lower_rows = jnp.take(current, starts + entries[0], axis=1 - time_axis)
    upper_rows = jnp.take(current, starts + child_rows + entries[1], axis=1 - time_axis)
    moved_rows = delay_rows(upper_rows, entries[2], child_rows, time_axis)
    return (lower_rows.astype(jnp.float32) + moved_rows.astype(jnp.float32)).astype(jnp.bfloat16)


def spectrum(delays, channels):
    row_count = delays.shape[0]
    length = delays.shape[1]
    fold_size = length // 128
    first_index = jnp.arange(fold_size, dtype=jnp.int32)
    lane_index = jnp.arange(128, dtype=jnp.int32)
    half_index = jnp.arange(64, dtype=jnp.int32)
    angle_one = (
        2.0
        * math.pi
        / fold_size
        * (first_index[:, None] * first_index[None, :] % fold_size).astype(jnp.float32)
    )
    cos_one = jnp.cos(angle_one).astype(jnp.bfloat16)
    sin_one = jnp.sin(angle_one).astype(jnp.bfloat16)
    angle_two = (
        2.0
        * math.pi
        / length
        * (first_index[:, None] * lane_index[None, :] % length).astype(jnp.float32)
    )
    twist_cos = jnp.cos(angle_two)
    twist_sin = jnp.sin(angle_two)
    angle_three = (
        2.0 * math.pi / 128 * (lane_index[:, None] * half_index[None, :] % 128).astype(jnp.float32)
    )
    cos_three = jnp.cos(angle_three).astype(jnp.bfloat16)
    sin_three = jnp.sin(angle_three).astype(jnp.bfloat16)
    series = delays.reshape(row_count, fold_size, 128)
    first_re = jnp.einsum("kn,rnm->rkm", cos_one, series, preferred_element_type=jnp.float32)
    first_im = -jnp.einsum("kn,rnm->rkm", sin_one, series, preferred_element_type=jnp.float32)
    twisted_re = (first_re * twist_cos + first_im * twist_sin).astype(jnp.bfloat16)
    twisted_im = (first_im * twist_cos - first_re * twist_sin).astype(jnp.bfloat16)
    out_re = jnp.einsum(
        "rkn,nj->rjk", twisted_re, cos_three, preferred_element_type=jnp.float32
    ) + jnp.einsum("rkn,nj->rjk", twisted_im, sin_three, preferred_element_type=jnp.float32)
    out_im = jnp.einsum(
        "rkn,nj->rjk", twisted_im, cos_three, preferred_element_type=jnp.float32
    ) - jnp.einsum("rkn,nj->rjk", twisted_re, sin_three, preferred_element_type=jnp.float32)
    power = (out_re * out_re + out_im * out_im) / (length * channels)
    return power.reshape(row_count, 64 * fold_size)


def local(samples, channel_order, merge_table):
    owners = lax.axis_size("sub")
    owner_index = lax.axis_index("sub")
    owned_rows = CH_DEV // 2
    quarter = CH_DEV // 4
    window = samples.shape[0]
    channels = samples.shape[1]
    ordered = jnp.take(samples, channel_order, axis=1).T.reshape(owners, CH_DEV, window)
    current = lax.all_to_all(ordered, "sub", split_axis=0, concat_axis=2, tiled=True).reshape(
        CH_DEV, window * owners
    )
    for level_num in range(1, LOCAL + 1):
        entries = lax.dynamic_slice_in_dim(
            merge_table[level_num - 1], owner_index * owned_rows, owned_rows, 1
        )
        current = merge_level(
            current, entries, max(1, 2 ** (level_num - 2)), 2 ** (level_num - 1), 1
        )
    block_index = jnp.zeros((), jnp.int32)
    for bit_num in range(owners.bit_length() - 1):
        level_num = LOCAL + bit_num + 1
        half_bit = owner_index >> bit_num & 1
        block_index = block_index * 2 + half_bit
        span_rows = owned_rows * 2 ** (bit_num + 1)
        child_rows = span_rows // 2
        subband = owner_index >> bit_num + 1
        entries = lax.dynamic_slice_in_dim(
            merge_table[level_num - 1],
            subband * span_rows + owned_rows * block_index,
            owned_rows,
            1,
        )
        kept_rows = lax.dynamic_slice_in_dim(current, half_bit * quarter, quarter, 0)
        sent_rows = lax.dynamic_slice_in_dim(current, (1 - half_bit) * quarter, quarter, 0)
        partner = from_partner(sent_rows, "sub", bit_num)
        row_base = quarter * block_index
        is_low = half_bit == 0
        lower_part = jnp.where(is_low, kept_rows, partner)
        upper_part = jnp.where(is_low, partner, kept_rows)
        lower_rows = jnp.take(lower_part, entries[0] - row_base, axis=0)
        upper_rows = jnp.take(upper_part, entries[1] - row_base, axis=0)
        moved_rows = delay_rows(upper_rows, entries[2], child_rows, 1)
        current = (lower_rows.astype(jnp.float32) + moved_rows.astype(jnp.float32)).astype(
            jnp.bfloat16
        )
    return spectrum(current[:, :SAMPLES], channels)


def solution(mesh):
    in_specs = (P(("groups", "sub"), None), P(), P())
    out_specs = P(("groups", "sub"), None)
    return jax.shard_map(local, mesh=mesh, in_specs=in_specs, out_specs=out_specs, check_vma=False)
```

profile of v0, /device:TPU:0, one launch (start us, length us, event | category | flops | bytes accessed | tf_op | source)
XLA Modules:
  0.0 79.7 jit_solution(5246893528105562320)
XLA Ops:
  0.0 0.8 compare_and_fusion.18
  0.8 1.3 %copy.4 = bf16[528,512]{0,1:T(8,128)(2,1)S(1)} copy(bf16[528,512]{1,0:T(8,128)(2,1)} %param.9) | data formatting | bytes 1081344 | tf_op args[0]
  2.1 2.0 %gather_fusion = bf16[512,528]{1,0:T(8,128)(2,1)S(1)} fusion(bf16[528,512]{0,1:T(8,128)(2,1)S(1)} %copy.4, s32[1024]{0:T(1024)S(1)} %pad_clamp_fusion.18), kind=kCustom, calls=%fused_computation.18 | custom fusion | bytes 1083392 | tf_op jit(solution)/shard_map/jit(_take)/gather | solution.py:93
  4.2 1.0 %broadcast_select_fusion = bf16[512,528]{1,0:T(8,128)(2,1)} fusion(bf16[512,528]{1,0:T(8,128)(2,1)S(1)} %gather_fusion, pred[512]{0:T(512)(128)(4,1)S(1)} %compare_and_fusion.18), kind=kLoop, calls=%fused_computation.29 | loop fusion | flops 270336 | bytes 1081856 | tf_op jit(solution)/shard_map/jit(_take)/select_n | solution.py:93
  5.2 7.4 %all-to-all-start = ((bf16[16,32,528]{2,1,0:T(8,128)(2,1)}), bf16[16,32,528]{2,1,0:T(8,128)(2,1)S(1)}, u32[]{:S(2)}, u32[]{:S(2)}) async-start(bf16[16,32,528]{2,1,0:T(8,128)(2,1)} %bitcast.10), calls=%async_computation | async-start | bytes 1310720 | tf_op jit(solution)/shard_map/all_to_all | solution.py:94
  12.6 0.7 copy-done
  14.3 14.9 %all-to-all-done = bf16[16,32,528]{2,1,0:T(8,128)(2,1)S(1)} async-done(((bf16[16,32,528]{2,1,0:T(8,128)(2,1)}), bf16[16,32,528]{2,1,0:T(8,128)(2,1)S(1)}, u32[]{:S(2)}, u32[]{:S(2)}) %all-to-all-start) | async-done | bytes 540704 | tf_op jit(solution)/shard_map/all_to_all | solution.py:94
  29.1 0.2 copy.5
  29.3 0.6 reshape.630
  30.0 0.7 gather_fusion.2
  30.7 0.7 gather_fusion.1
  31.7 0.2 add_convert_fusion.7
  31.9 0.7 gather_fusion.4
  32.6 0.7 gather_fusion.3
  33.6 0.2 add_convert_fusion.6
  33.8 0.7 gather_fusion.6
  34.5 0.7 gather_fusion.5
  36.0 0.7 gather_fusion.8
  36.7 0.7 gather_fusion.7
  38.3 0.2 add_convert_fusion.4
  38.5 0.7 gather_fusion.10
  39.2 0.7 gather_fusion.9
  41.0 0.2 add_convert_fusion.3
  41.2 0.2 collective-permute-start
  41.5 1.2 %collective-permute-done = bf16[8,8448]{1,0:T(8,128)(2,1)S(1)} collective-permute-done((bf16[8,8448]{1,0:T(8,128)(2,1)S(1)}, bf16[8,8448]{1,0:T(8,128)(2,1)S(1)}, u32[]{:S(2)}, u32[]{:S(2)}) %collective-permute-start) | collective-permute-done | bytes 135200 | tf_op jit(solution)/shard_map/ppermute | solution.py:19
  42.7 0.7 gather_fusion.12
  44.8 0.7 gather_fusion.11
  45.8 1.3 %collective-permute-start.1 = (bf16[8,8448]{1,0:T(8,128)(2,1)S(1)}, bf16[8,8448]{1,0:T(8,128)(2,1)S(1)}, u32[]{:S(2)}, u32[]{:S(2)}) collective-permute-start(bf16[8,8448]{1,0:T(8,128)(2,1)S(1)} %constant_dynamic-slice_fusion.5), channel_id=1, source_target_pairs={{0,2},{2,0},{1,3},{3,1},{4,6},{6,4},{5,7},{7,5},{8,10},{10,8},{9,1... | collective-permute-start | bytes 405512 | tf_op jit(solution)/shard_map/ppermute | solution.py:19
  47.1 4.4 %collective-permute-done.1 = bf16[8,8448]{1,0:T(8,128)(2,1)S(1)} collective-permute-done((bf16[8,8448]{1,0:T(8,128)(2,1)S(1)}, bf16[8,8448]{1,0:T(8,128)(2,1)S(1)}, u32[]{:S(2)}, u32[]{:S(2)}) %collective-permute-start.1) | collective-permute-done | bytes 135200 | tf_op jit(solution)/shard_map/ppermute | solution.py:19
  51.6 0.7 gather_fusion.14
  54.0 0.7 gather_fusion.13
  54.9 2.3 %collective-permute-start.2 = (bf16[8,8448]{1,0:T(8,128)(2,1)S(1)}, bf16[8,8448]{1,0:T(8,128)(2,1)S(1)}, u32[]{:S(2)}, u32[]{:S(2)}) collective-permute-start(bf16[8,8448]{1,0:T(8,128)(2,1)S(1)} %constant_dynamic-slice_fusion.3), channel_id=1, source_target_pairs={{0,4},{4,0},{1,5},{5,1},{2,6},{6,2},{3,7},{7,3},{8,12},{12,8},{9,1... | collective-permute-start | bytes 405512 | tf_op jit(solution)/shard_map/ppermute | solution.py:19
  57.2 3.2 %collective-permute-done.2 = bf16[8,8448]{1,0:T(8,128)(2,1)S(1)} collective-permute-done((bf16[8,8448]{1,0:T(8,128)(2,1)S(1)}, bf16[8,8448]{1,0:T(8,128)(2,1)S(1)}, u32[]{:S(2)}, u32[]{:S(2)}) %collective-permute-start.2) | collective-permute-done | bytes 135200 | tf_op jit(solution)/shard_map/ppermute | solution.py:19
  60.5 0.7 gather_fusion.16
  63.2 0.7 gather_fusion.15
  63.9 0.4 add_convert_fusion
  64.3 2.5 %collective-permute-start.3 = (bf16[8,8448]{1,0:T(8,128)(2,1)S(1)}, bf16[8,8448]{1,0:T(8,128)(2,1)S(1)}, u32[]{:S(2)}, u32[]{:S(2)}) collective-permute-start(bf16[8,8448]{1,0:T(8,128)(2,1)S(1)} %constant_dynamic-slice_fusion.1), channel_id=1, source_target_pairs={{0,8},{8,0},{1,9},{9,1},{2,10},{10,2},{3,11},{11,3},{4,12},{12,4},... | collective-permute-start | bytes 405512 | tf_op jit(solution)/shard_map/ppermute | solution.py:19
  67.0 5.6 %collective-permute-done.3 = bf16[8,8448]{1,0:T(8,128)(2,1)S(1)} collective-permute-done((bf16[8,8448]{1,0:T(8,128)(2,1)S(1)}, bf16[8,8448]{1,0:T(8,128)(2,1)S(1)}, u32[]{:S(2)}, u32[]{:S(2)}) %collective-permute-start.3) | collective-permute-done | bytes 135200 | tf_op jit(solution)/shard_map/ppermute | solution.py:19
  72.6 0.7 gather_fusion.18
  75.5 0.7 gather_fusion.17
  76.2 0.2 fusion.6
  76.4 0.3 convolution_bitcast_fusion
  76.8 0.4 add_convert_fusion.8
  77.2 0.4 fusion.39
  77.6 0.4 fusion.37
  78.0 0.4 fusion.1
  78.4 0.4 fusion.5
  78.8 0.9 %reshape.632 = f32[16,4096]{1,0:T(8,128)} reshape(f32[16,64,64]{2,1,0:T(8,128)S(1)} %fusion.5) | data formatting | bytes 524288 | tf_op jit(solution)/shard_map/reshape | solution.py:83
  (131 shorter events, 11.6 us)
Async XLA Ops:
  0.0 0.8 copy-start.1
  5.2 24.0 %all-to-all-start = ((bf16[16,32,528]{2,1,0:T(8,128)(2,1)}), bf16[16,32,528]{2,1,0:T(8,128)(2,1)S(1)}, u32[]{:S(2)}, u32[]{:S(2)}) async-start(bf16[16,32,528]{2,1,0:T(8,128)(2,1)} %bitcast.10), calls=%async_computation | async-start | bytes 1310720 | tf_op jit(solution)/shard_map/all_to_all | solution.py:94
  12.6 0.8 copy-start
  41.2 1.4 %collective-permute-start = (bf16[8,8448]{1,0:T(8,128)(2,1)S(1)}, bf16[8,8448]{1,0:T(8,128)(2,1)S(1)}, u32[]{:S(2)}, u32[]{:S(2)}) collective-permute-start(bf16[8,8448]{1,0:T(8,128)(2,1)S(1)} %constant_dynamic-slice_fusion.7), channel_id=1, source_target_pairs={{0,1},{1,0},{2,3},{3,2},{4,5},{5,4},{6,7},{7,6},{8,9},{9,8},{10,11... | collective-permute-start | bytes 405512 | tf_op jit(solution)/shard_map/ppermute | solution.py:19
  45.8 5.7 %collective-permute-start.1 = (bf16[8,8448]{1,0:T(8,128)(2,1)S(1)}, bf16[8,8448]{1,0:T(8,128)(2,1)S(1)}, u32[]{:S(2)}, u32[]{:S(2)}) collective-permute-start(bf16[8,8448]{1,0:T(8,128)(2,1)S(1)} %constant_dynamic-slice_fusion.5), channel_id=1, source_target_pairs={{0,2},{2,0},{1,3},{3,1},{4,6},{6,4},{5,7},{7,5},{8,10},{10,8},{9,1... | collective-permute-start | bytes 405512 | tf_op jit(solution)/shard_map/ppermute | solution.py:19
  54.9 5.5 %collective-permute-start.2 = (bf16[8,8448]{1,0:T(8,128)(2,1)S(1)}, bf16[8,8448]{1,0:T(8,128)(2,1)S(1)}, u32[]{:S(2)}, u32[]{:S(2)}) collective-permute-start(bf16[8,8448]{1,0:T(8,128)(2,1)S(1)} %constant_dynamic-slice_fusion.3), channel_id=1, source_target_pairs={{0,4},{4,0},{1,5},{5,1},{2,6},{6,2},{3,7},{7,3},{8,12},{12,8},{9,1... | collective-permute-start | bytes 405512 | tf_op jit(solution)/shard_map/ppermute | solution.py:19
  64.3 8.3 %collective-permute-start.3 = (bf16[8,8448]{1,0:T(8,128)(2,1)S(1)}, bf16[8,8448]{1,0:T(8,128)(2,1)S(1)}, u32[]{:S(2)}, u32[]{:S(2)}) collective-permute-start(bf16[8,8448]{1,0:T(8,128)(2,1)S(1)} %constant_dynamic-slice_fusion.1), channel_id=1, source_target_pairs={{0,8},{8,0},{1,9},{9,1},{2,10},{10,2},{3,11},{11,3},{4,12},{12,4},... | collective-permute-start | bytes 405512 | tf_op jit(solution)/shard_map/ppermute | solution.py:19
where the time goes:
time: 80.1 us; the launch traced here: 79.7 us
  waiting for transfers between devices  29.3 us (37%)
  local copies, waits for them, and re-layouts  24.4 us (30%)
  starting transfers between devices  13.7 us (17%)
  other arithmetic  9.1 us (11%)
  matrix products  2.37 us (3%)
  between operations  0.9 us (1%)
    all_to_all x1, waiting for transfers between devices, local(): lax.all_to_all(ordered, 'sub', split_axis=0, concat_axis=2, tiled=True)  14.9 us
    ppermute x4, waiting for transfers between devices, from_partner(): return lax.ppermute(block, axis, route)  14.4 us
    all_to_all x1, starting transfers between devices, local(): lax.all_to_all(ordered, 'sub', split_axis=0, concat_axis=2, tiled=True)  7.39 us
    ppermute x4, starting transfers between devices, from_partner(): return lax.ppermute(block, axis, route)  6.35 us
    slice x37, local copies, waits for them, and re-layouts, delay_rows(): rolled = jnp.pad(moved[:, offset:], ((0, 0), (0, offset)))  4.93 us
    select_n x28, other arithmetic, delay_rows(): moved = jnp.where(flagged, rolled, moved)  3.93 us
    gather x5, local copies, waits for them, and re-layouts, merge_level(): jnp.take(current, starts + child_rows + entries[1], axis=1 - time_axis)  3.6 us
    gather x5, local copies, waits for them, and re-layouts, merge_level(): lower_rows = jnp.take(current, starts + entries[0], axis=1 - time_axis)  3.59 us
  transfers between devices with their start and end apart: 5, of which 5 were waited for; matrix products, arithmetic and copies ran while one was open for 1% of the time, Pallas kernels for 0%

commit v1 on v0

--- a/solution.py
+++ b/solution.py
@@ -91,9 +91,10 @@
     window = samples.shape[0]
     channels = samples.shape[1]
     ordered = jnp.take(samples, channel_order, axis=1).T.reshape(owners, CH_DEV, window)
-    current = lax.all_to_all(ordered, "sub", split_axis=0, concat_axis=2, tiled=True).reshape(
-        CH_DEV, window * owners
-    )
+    current = jnp.concatenate(
+        lax.all_to_all(jnp.stack(jnp.split(ordered, lax.axis_size("sub"), axis=0)), "sub", 0, 0),
+        axis=2,
+    ).reshape(CH_DEV, window * owners)
     for level_num in range(1, LOCAL + 1):
         entries = lax.dynamic_slice_in_dim(
             merge_table[level_num - 1], owner_index * owned_rows, owned_rows, 1

time: 80.1 us -> 90.2 us (1.13)
  local copies, waits for them, and re-layouts: 24.4 us -> 34.7 us
  other arithmetic: 9.1 us -> 8.03 us
    unnamed x6 -> x25, local copies, waits for them, and re-layouts: 2.11 us -> 11.6 us
    another operation x0 -> x2, local copies, waits for them, and re-layouts: none -> 1.26 us  [the longest x1 0.65 us: local(): current = jnp.concatenate(lax.all_to_all(jnp.stack(jnp.split(ordered, lax...]
    slice x37 -> x38, local copies, waits for them, and re-layouts: 4.93 us -> 4.99 us  [delay_rows(): rolled = jnp.pad(moved[:, offset:], ((0, 0), (0, offset)))]
where the time goes in v1:
time: 90.2 us; the launch traced here: 89.9 us
  local copies, waits for them, and re-layouts  34.7 us (38%)
  waiting for transfers between devices  29.8 us (33%)
  starting transfers between devices  13.9 us (15%)
  other arithmetic  8.03 us (9%)
  matrix products  2.37 us (3%)
  between operations  1.09 us (1%)
    all_to_all x1, waiting for transfers between devices, local(): lax.all_to_all(jnp.stack(jnp.split(ordered, lax.axis_size('sub'), axis=0)...  15.5 us
    ppermute x4, waiting for transfers between devices, from_partner(): return lax.ppermute(block, axis, route)  14.3 us
    unnamed x25, local copies, waits for them, and re-layouts  11.6 us
    all_to_all x1, starting transfers between devices, local(): lax.all_to_all(jnp.stack(jnp.split(ordered, lax.axis_size('sub'), axis=0)...  7.52 us
    ppermute x4, starting transfers between devices, from_partner(): return lax.ppermute(block, axis, route)  6.35 us
    slice x38, local copies, waits for them, and re-layouts, delay_rows(): rolled = jnp.pad(moved[:, offset:], ((0, 0), (0, offset)))  4.99 us
    select_n x28, other arithmetic, delay_rows(): moved = jnp.where(flagged, rolled, moved)  3.93 us
    gather x5, local copies, waits for them, and re-layouts, merge_level(): jnp.take(current, starts + child_rows + entries[1], axis=1 - time_axis)  3.6 us
  transfers between devices with their start and end apart: 5, of which 5 were waited for; matrix products, arithmetic and copies ran while one was open for 1% of the time, Pallas kernels for 0%

profile of v1, /device:TPU:0, one launch (start us, length us, event | category | flops | bytes accessed | tf_op | source)
XLA Modules:
  0.0 89.9 jit_solution(11549918489755444453)
XLA Ops:
  0.0 0.8 compare_select_fusion
  0.8 1.3 %copy.5 = bf16[528,512]{0,1:T(8,128)(2,1)S(1)} copy(bf16[528,512]{1,0:T(8,128)(2,1)} %param.9) | data formatting | bytes 1081344 | tf_op args[0]
  2.1 2.0 %gather_fusion = bf16[512,528]{1,0:T(8,128)(2,1)S(1)} fusion(bf16[528,512]{0,1:T(8,128)(2,1)S(1)} %copy.5, s32[1024]{0:T(1024)S(1)} %pad_clamp_fusion.18), kind=kCustom, calls=%fused_computation.18 | custom fusion | bytes 1083392 | tf_op jit(solution)/shard_map/jit(_take)/gather | solution.py:93
  4.3 0.6 fusion.22
  5.6 0.6 fusion.20
  6.2 0.6 fusion.19
  6.8 0.6 fusion.18
  7.4 0.6 fusion.17
  8.0 0.6 fusion.16
  8.6 0.6 fusion.15
  9.3 0.6 fusion.14
  9.9 0.6 fusion.13
  10.5 0.6 fusion.12
  11.1 0.6 fusion.11
  11.7 0.6 fusion.10
  12.4 0.6 fusion.9
  13.0 0.6 fusion.8
  13.6 0.6 fusion.7
  14.2 7.5 %all-to-all-start = ((bf16[16,1,32,528]{3,2,1,0:T(8,128)(2,1)}), bf16[16,1,32,528]{3,2,1,0:T(8,128)(2,1)S(1)}, u32[]{:S(2)}, u32[]{:S(2)}) async-start(bf16[16,1,32,528]{3,2,1,0:T(8,128)(2,1)} %fusion.7), calls=%async_computation | async-start | bytes 1310720 | tf_op jit(solution)/shard_map/all_to_all | solution.py:95
  22.8 15.5 %all-to-all-done = bf16[16,1,32,528]{3,2,1,0:T(8,128)(2,1)S(1)} async-done(((bf16[16,1,32,528]{3,2,1,0:T(8,128)(2,1)}), bf16[16,1,32,528]{3,2,1,0:T(8,128)(2,1)S(1)}, u32[]{:S(2)}, u32[]{:S(2)}) %all-to-all-start) | async-done | bytes 540704 | tf_op jit(solution)/shard_map/all_to_all | solution.py:95
  38.5 0.6 reshape_reshape.3
  39.2 0.7 gather_fusion.2
  40.1 0.7 gather_fusion.1
  41.1 0.7 gather_fusion.4
  42.0 0.7 gather_fusion.3
  43.0 0.7 gather_fusion.6
  44.2 0.7 gather_fusion.5
  45.2 0.7 gather_fusion.8
  46.7 0.7 gather_fusion.7
  47.6 0.7 gather_fusion.10
  49.5 0.7 gather_fusion.9
  50.7 1.1 %collective-permute-done = bf16[8,8448]{1,0:T(8,128)(2,1)S(1)} collective-permute-done((bf16[8,8448]{1,0:T(8,128)(2,1)S(1)}, bf16[8,8448]{1,0:T(8,128)(2,1)S(1)}, u32[]{:S(2)}, u32[]{:S(2)}) %collective-permute-start) | collective-permute-done | bytes 135200 | tf_op jit(solution)/shard_map/ppermute | solution.py:19
  51.9 0.7 gather_fusion.12
  54.0 0.7 gather_fusion.11
  54.9 1.3 %collective-permute-start.1 = (bf16[8,8448]{1,0:T(8,128)(2,1)S(1)}, bf16[8,8448]{1,0:T(8,128)(2,1)S(1)}, u32[]{:S(2)}, u32[]{:S(2)}) collective-permute-start(bf16[8,8448]{1,0:T(8,128)(2,1)S(1)} %constant_dynamic-slice_fusion.5), channel_id=1, source_target_pairs={{0,2},{2,0},{1,3},{3,1},{4,6},{6,4},{5,7},{7,5},{8,10},{10,8},{9,1... | collective-permute-start | bytes 405512 | tf_op jit(solution)/shard_map/ppermute | solution.py:19
  56.3 4.4 %collective-permute-done.1 = bf16[8,8448]{1,0:T(8,128)(2,1)S(1)} collective-permute-done((bf16[8,8448]{1,0:T(8,128)(2,1)S(1)}, bf16[8,8448]{1,0:T(8,128)(2,1)S(1)}, u32[]{:S(2)}, u32[]{:S(2)}) %collective-permute-start.1) | collective-permute-done | bytes 135200 | tf_op jit(solution)/shard_map/ppermute | solution.py:19
  60.7 0.7 gather_fusion.14
  63.1 0.7 gather_fusion.13
  64.1 2.3 %collective-permute-start.2 = (bf16[8,8448]{1,0:T(8,128)(2,1)S(1)}, bf16[8,8448]{1,0:T(8,128)(2,1)S(1)}, u32[]{:S(2)}, u32[]{:S(2)}) collective-permute-start(bf16[8,8448]{1,0:T(8,128)(2,1)S(1)} %constant_dynamic-slice_fusion.3), channel_id=1, source_target_pairs={{0,4},{4,0},{1,5},{5,1},{2,6},{6,2},{3,7},{7,3},{8,12},{12,8},{9,1... | collective-permute-start | bytes 405512 | tf_op jit(solution)/shard_map/ppermute | solution.py:19
  66.4 3.2 %collective-permute-done.2 = bf16[8,8448]{1,0:T(8,128)(2,1)S(1)} collective-permute-done((bf16[8,8448]{1,0:T(8,128)(2,1)S(1)}, bf16[8,8448]{1,0:T(8,128)(2,1)S(1)}, u32[]{:S(2)}, u32[]{:S(2)}) %collective-permute-start.2) | collective-permute-done | bytes 135200 | tf_op jit(solution)/shard_map/ppermute | solution.py:19
  69.6 0.7 gather_fusion.16
  72.3 0.7 gather_fusion.15
  73.4 2.5 %collective-permute-start.3 = (bf16[8,8448]{1,0:T(8,128)(2,1)S(1)}, bf16[8,8448]{1,0:T(8,128)(2,1)S(1)}, u32[]{:S(2)}, u32[]{:S(2)}) collective-permute-start(bf16[8,8448]{1,0:T(8,128)(2,1)S(1)} %constant_dynamic-slice_fusion.1), channel_id=1, source_target_pairs={{0,8},{8,0},{1,9},{9,1},{2,10},{10,2},{3,11},{11,3},{4,12},{12,4},... | collective-permute-start | bytes 405512 | tf_op jit(solution)/shard_map/ppermute | solution.py:19
  76.1 5.6 %collective-permute-done.3 = bf16[8,8448]{1,0:T(8,128)(2,1)S(1)} collective-permute-done((bf16[8,8448]{1,0:T(8,128)(2,1)S(1)}, bf16[8,8448]{1,0:T(8,128)(2,1)S(1)}, u32[]{:S(2)}, u32[]{:S(2)}) %collective-permute-start.3) | collective-permute-done | bytes 135200 | tf_op jit(solution)/shard_map/ppermute | solution.py:19
  81.8 0.7 gather_fusion.18
  84.6 0.7 copy-done
  85.3 0.7 gather_fusion.17
  89.0 0.9 reshape.660
  (150 shorter events, 16.7 us)
Async XLA Ops:
  0.0 0.8 copy-start.3
  14.2 7.5 %copy-start.2 = (s32[9,3,256]{2,1,0:T(4,128)S(1)}, s32[9,3,256]{2,1,0:T(4,128)}, u32[]{:S(2)}) copy-start(s32[9,3,256]{2,1,0:T(4,128)} %param.11) | copy-start | bytes 82948
  14.2 24.1 %all-to-all-start = ((bf16[16,1,32,528]{3,2,1,0:T(8,128)(2,1)}), bf16[16,1,32,528]{3,2,1,0:T(8,128)(2,1)S(1)}, u32[]{:S(2)}, u32[]{:S(2)}) async-start(bf16[16,1,32,528]{3,2,1,0:T(8,128)(2,1)} %fusion.7), calls=%async_computation | async-start | bytes 1310720 | tf_op jit(solution)/shard_map/all_to_all | solution.py:95
  50.4 1.4 %collective-permute-start = (bf16[8,8448]{1,0:T(8,128)(2,1)S(1)}, bf16[8,8448]{1,0:T(8,128)(2,1)S(1)}, u32[]{:S(2)}, u32[]{:S(2)}) collective-permute-start(bf16[8,8448]{1,0:T(8,128)(2,1)S(1)} %constant_dynamic-slice_fusion.7), channel_id=1, source_target_pairs={{0,1},{1,0},{2,3},{3,2},{4,5},{5,4},{6,7},{7,6},{8,9},{9,8},{10,11... | collective-permute-start | bytes 405512 | tf_op jit(solution)/shard_map/ppermute | solution.py:19
  54.9 5.7 %collective-permute-start.1 = (bf16[8,8448]{1,0:T(8,128)(2,1)S(1)}, bf16[8,8448]{1,0:T(8,128)(2,1)S(1)}, u32[]{:S(2)}, u32[]{:S(2)}) collective-permute-start(bf16[8,8448]{1,0:T(8,128)(2,1)S(1)} %constant_dynamic-slice_fusion.5), channel_id=1, source_target_pairs={{0,2},{2,0},{1,3},{3,1},{4,6},{6,4},{5,7},{7,5},{8,10},{10,8},{9,1... | collective-permute-start | bytes 405512 | tf_op jit(solution)/shard_map/ppermute | solution.py:19
  64.1 5.5 %collective-permute-start.2 = (bf16[8,8448]{1,0:T(8,128)(2,1)S(1)}, bf16[8,8448]{1,0:T(8,128)(2,1)S(1)}, u32[]{:S(2)}, u32[]{:S(2)}) collective-permute-start(bf16[8,8448]{1,0:T(8,128)(2,1)S(1)} %constant_dynamic-slice_fusion.3), channel_id=1, source_target_pairs={{0,4},{4,0},{1,5},{5,1},{2,6},{6,2},{3,7},{7,3},{8,12},{12,8},{9,1... | collective-permute-start | bytes 405512 | tf_op jit(solution)/shard_map/ppermute | solution.py:19
  73.4 8.3 %collective-permute-start.3 = (bf16[8,8448]{1,0:T(8,128)(2,1)S(1)}, bf16[8,8448]{1,0:T(8,128)(2,1)S(1)}, u32[]{:S(2)}, u32[]{:S(2)}) collective-permute-start(bf16[8,8448]{1,0:T(8,128)(2,1)S(1)} %constant_dynamic-slice_fusion.1), channel_id=1, source_target_pairs={{0,8},{8,0},{1,9},{9,1},{2,10},{10,2},{3,11},{11,3},{4,12},{12,4},... | collective-permute-start | bytes 405512 | tf_op jit(solution)/shard_map/ppermute | solution.py:19
  84.6 0.7 copy-start
  85.3 1.0 %copy-start.1 = (bf16[16,8448]{1,0:T(8,128)(2,1)S(1)}, bf16[16,8448]{1,0:T(8,128)(2,1)}, u32[]{:S(2)}) copy-start(bf16[16,8448]{1,0:T(8,128)(2,1)} %copy-done) | copy-start | bytes 811012
  85.3 1.0 %slice-start = ((bf16[16,8448]{1,0:T(8,128)(2,1)}), bf16[16,8320]{1,0:T(8,128)(2,1)S(1)}, s32[]{:S(2)}) async-start(bf16[16,8448]{1,0:T(8,128)(2,1)} %copy-done), calls=%async_computation.1 | async-start | bytes 532480 | tf_op jit(solution)/shard_map/slice | solution.py:27
